TPU v7x, 32 devices: a whole 2x2x4 slice. The times are simulated.
32 devices in a mesh: seq: 8 (over z, x), ch: 4 (over y, core).
Axes of the slice: x: 2, y: 2, z: 4, core: 2. Of those that a mesh axis runs over, the one named last changes fastest.
Arguments:
- query_raw: bfloat16 [1024, 2048], P('seq', 'ch'), may hold values from -6 to 6
- key_raw: bfloat16 [1024, 2048], P('seq', 'ch'), may hold values from -6 to 6
- value_raw: bfloat16 [1024, 2048], P('seq', 'ch'), may hold values from -6 to 6
- featurizer: float32 [3, 7, 2048], P(None, None, 'ch'), may hold values from -2 to 2
- filter_taps: bfloat16 [1024, 2048], P(('seq', 'ch')), may hold values from -2.5 to 2.5
- cotangent: bfloat16 [1024, 2048], P('seq', 'ch'), may hold values from -6 to 6
Outputs:
- mixed: bfloat16 [1024, 2048], P('seq', 'ch')
- query_grad: bfloat16 [1024, 2048], P('seq', 'ch')
- key_grad: bfloat16 [1024, 2048], P('seq', 'ch')
- value_grad: bfloat16 [1024, 2048], P('seq', 'ch')
- filter_grad: float32 [1024, 2048], P(('seq', 'ch'))
- featurizer_grad: float32 [3, 7, 2048], P(None, None, 'ch')
All inputs are finite; a program needn't handle non-finite values.
Results may differ from a plain program's by a relative error of at most 0.0085.
Values may be sent and summed in bfloat16 or wider, within the bound.
A program may use at most 64 MiB of HBM per device.

v0:
```python
import functools
import math

import jax
import jax.numpy as jnp
import numpy as np
from jax import lax
from jax.experimental import pallas as pl
from jax.experimental.pallas import tpu as pltpu
from jax.sharding import PartitionSpec as P

TAPS = 7


exact_mode = lax.Precision.HIGHEST


def passed_along(value, axis, steps):
    count = lax.axis_size(axis)
    initial, last = (max(0, -steps), min(count, count - steps))
    return lax.ppermute(value, axis, [(source, source + steps) for source in range(initial, last)])


def spectrum_tables(half_rows, tile_width):
    full_rows = 2 * half_rows
    length_full = full_rows * tile_width
    row_index = jnp.arange(full_rows, dtype=jnp.int32)
    col_index = jnp.arange(tile_width, dtype=jnp.int32)
    outer_angle = (
        2.0
        * math.pi
        / full_rows
        * (row_index[:, None] * row_index[None, :] % full_rows).astype(jnp.float32)
    )
    twist_angle = (
        2.0
        * math.pi
        / length_full
        * (row_index[:, None] * col_index[None, :] % length_full).astype(jnp.float32)
    )
    inner_angle = (
        2.0
        * math.pi
        / tile_width
        * (col_index[:, None] * col_index[None, :] % tile_width).astype(jnp.float32)
    )
    return (
        jnp.cos(outer_angle),
        -jnp.sin(outer_angle),
        jnp.cos(twist_angle),
        -jnp.sin(twist_angle),
        jnp.cos(inner_angle),
        -jnp.sin(inner_angle),
    )


def right_product(left, table):
    return jnp.einsum("ckm,mj->ckj", left, table, precision=exact_mode)


def to_spectrum(signal, tables):
    outer_re, outer_im, twist_re, twist_im, inner_re, inner_im = tables
    half_rows = outer_re.shape[0] // 2
    tile_width = inner_re.shape[0]
    blocks = signal.reshape(signal.shape[0], half_rows, tile_width)
    section_re = jnp.einsum("kn,cnm->ckm", outer_re[:, :half_rows], blocks, precision=exact_mode)
    section_im = jnp.einsum("kn,cnm->ckm", outer_im[:, :half_rows], blocks, precision=exact_mode)
    turned_re = section_re * twist_re - section_im * twist_im
    turned_im = section_re * twist_im + section_im * twist_re
    spec_re = right_product(turned_re, inner_re) - right_product(turned_im, inner_im)
    spec_im = right_product(turned_re, inner_im) + right_product(turned_im, inner_re)
    return (spec_re, spec_im)


def from_spectrum(spectrum, tables):
    outer_re, outer_im, twist_re, twist_im, inner_re, inner_im = tables
    half_rows = outer_re.shape[0] // 2
    tile_width = inner_re.shape[0]
    spec_re, spec_im = spectrum
    back_re = right_product(spec_re, inner_re) + right_product(spec_im, inner_im)
    back_im = right_product(spec_im, inner_re) - right_product(spec_re, inner_im)
    untwist_re = back_re * twist_re + back_im * twist_im
    untwist_im = back_im * twist_re - back_re * twist_im
    signal = jnp.einsum("nk,ckm->cnm", outer_re[:half_rows], untwist_re, precision=exact_mode)
    signal = signal + jnp.einsum(
        "nk,ckm->cnm", outer_im[:half_rows], untwist_im, precision=exact_mode
    )
    return signal.reshape(signal.shape[0], half_rows * tile_width) / (2.0 * half_rows * tile_width)


def times_spectrum(first, second):
    return (
        first[0] * second[0] - first[1] * second[1],
        first[0] * second[1] + first[1] * second[0],
    )


def conj_times(first, second):
    return (
        first[0] * second[0] + first[1] * second[1],
        first[0] * second[1] - first[1] * second[0],
    )


def featurize(padded, weight, tok_rows):
    total = jnp.zeros((tok_rows, padded.shape[1]), jnp.float32)
    for lag_index in range(TAPS):
        start = TAPS - 1 - lag_index
        total = total + weight[lag_index][None, :] * padded[start : start + tok_rows]
    return total


def unfeaturize(extended, weight, tok_rows):
    total = jnp.zeros((tok_rows, extended.shape[1]), jnp.float32)
    for lag_index in range(TAPS):
        total = total + weight[lag_index][None, :] * extended[lag_index : lag_index + tok_rows]
    return total


def weight_terms(grad, padded, tok_rows):
    terms = []
    for lag_index in range(TAPS):
        start = TAPS - 1 - lag_index
        terms.append(jnp.sum(grad * padded[start : start + tok_rows], axis=0))
    return jnp.stack(terms)


def on_device_large(query_raw, key_raw, value_raw, featurizer, filter_taps, cotangent):
    tok_rows = query_raw.shape[0]
    lag_rows = TAPS - 1
    cut_start = tok_rows - lag_rows
    seq_count = lax.axis_size("seq")
    ch_count = lax.axis_size("ch")
    rim_query, rim_key, rim_value = passed_along(
        (query_raw[cut_start:], key_raw[cut_start:], value_raw[cut_start:]), "seq", 1
    )
    padded_query = jnp.concatenate([rim_query, query_raw], axis=0).astype(jnp.float32)
    padded_key = jnp.concatenate([rim_key, key_raw], axis=0).astype(jnp.float32)
    padded_value = jnp.concatenate([rim_value, value_raw], axis=0).astype(jnp.float32)
    feat_query = featurize(padded_query, featurizer[0], tok_rows)
    feat_key = featurize(padded_key, featurizer[1], tok_rows)
    feat_value = featurize(padded_value, featurizer[2], tok_rows)
    mixer = (feat_key * feat_value).astype(jnp.bfloat16)
    mix_cols = lax.all_to_all(mixer.T, "seq", split_axis=0, concat_axis=1, tiled=True)
    chan_total, row_part = (filter_taps.shape[1], filter_taps.shape[0])
    block_width = chan_total // (seq_count * ch_count)
    ordered = filter_taps.T.reshape(ch_count, seq_count, block_width, row_part)
    ordered = jnp.transpose(ordered, (1, 0, 2, 3)).reshape(chan_total, row_part)
    taps_cols = lax.all_to_all(ordered, ("seq", "ch"), split_axis=0, concat_axis=1, tiled=True)
    length_full = mix_cols.shape[1]
    tables = spectrum_tables(length_full // 128, 128)
    mix_spec = to_spectrum(mix_cols.astype(jnp.float32), tables)
    taps_spec = to_spectrum(taps_cols.astype(jnp.float32), tables)
    conv_cols = from_spectrum(times_spectrum(taps_spec, mix_spec), tables).astype(jnp.bfloat16)
    conv_rows = lax.all_to_all(conv_cols, "seq", split_axis=1, concat_axis=0, tiled=True).T
    conv_float = conv_rows.astype(jnp.float32)
    mixed = (feat_query * conv_float).astype(jnp.bfloat16)
    upstream = cotangent.astype(jnp.float32)
    gate = (upstream * feat_query).astype(jnp.bfloat16)
    gate_cols = lax.all_to_all(gate.T, "seq", split_axis=0, concat_axis=1, tiled=True)
    gate_spec = to_spectrum(gate_cols.astype(jnp.float32), tables)
    scale = length_full ** (-0.5)
    mix_grad_cols = from_spectrum(conj_times(taps_spec, gate_spec), tables).astype(jnp.bfloat16)
    taps_grad_cols = from_spectrum(conj_times(mix_spec, gate_spec), tables) * scale
    mix_back = lax.all_to_all(mix_grad_cols, "seq", split_axis=1, concat_axis=0, tiled=True)
    mix_grad_float = mix_back.T.astype(jnp.float32)
    joint_back = lax.all_to_all(
        taps_grad_cols, ("seq", "ch"), split_axis=1, concat_axis=0, tiled=True
    )
    block_width = joint_back.shape[0] // (seq_count * ch_count)
    row_part = joint_back.shape[1]
    unordered = joint_back.reshape(seq_count, ch_count, block_width, row_part)
    unordered = jnp.transpose(unordered, (1, 0, 2, 3)).reshape(joint_back.shape[0], row_part)
    filter_grad = unordered.T
    query_feat_grad = upstream * conv_float
    key_feat_grad = mix_grad_float * feat_value
    value_feat_grad = mix_grad_float * feat_key
    next_query, next_key, next_value = passed_along(
        (query_feat_grad[:lag_rows], key_feat_grad[:lag_rows], value_feat_grad[:lag_rows]),
        "seq",
        -1,
    )
    query_grad = unfeaturize(
        jnp.concatenate([query_feat_grad, next_query], axis=0), featurizer[0], tok_rows
    )
    key_grad = unfeaturize(
        jnp.concatenate([key_feat_grad, next_key], axis=0), featurizer[1], tok_rows
    )
    value_grad = unfeaturize(
        jnp.concatenate([value_feat_grad, next_value], axis=0), featurizer[2], tok_rows
    )
    partial_terms = jnp.stack(
        [
            weight_terms(query_feat_grad, padded_query, tok_rows),
            weight_terms(key_feat_grad, padded_key, tok_rows),
            weight_terms(value_feat_grad, padded_value, tok_rows),
        ]
    )
    featurizer_grad = lax.psum(partial_terms, "seq") * scale
    return (
        mixed,
        query_grad.astype(jnp.bfloat16),
        key_grad.astype(jnp.bfloat16),
        value_grad.astype(jnp.bfloat16),
        filter_grad,
        featurizer_grad,
    )


LANES = 128
HALO = 16
STEP = 32
MESH = pl.DeviceIdType.MESH


def angle_tables(length):
    full = 2 * length
    col = np.arange(length)
    coarse = np.arange(length // STEP + 1) * STEP
    coarse = 2.0 * np.pi / full * ((coarse[:, None] * col[None, :LANES]) % full)
    fine = 2.0 * np.pi / full * ((np.arange(STEP)[:, None] * col[None, :]) % full)
    return [
        np.asarray(part, np.float32)
        for part in (np.cos(coarse), np.sin(coarse), np.cos(fine), np.sin(fine))
    ]


def split_parts(value):
    high = value.astype(jnp.bfloat16)
    return high, (value - high.astype(jnp.float32)).astype(jnp.bfloat16)


def matmul(left, right):
    return jnp.dot(left, right, preferred_element_type=jnp.float32)


def swapped(value):
    return pltpu.roll(value, LANES // 2, axis=1)


def low_lanes(rows):
    return lax.broadcasted_iota(jnp.int32, (rows, LANES), 1) < LANES // 2


def operator_kernel(
    dims,
    q_ref, k_ref, v_ref, w_ref, taps_ref, cot_ref, ac_ref, as_ref, bc_ref, bs_ref,
    mixed_ref, qg_ref, kg_ref, vg_ref, fgrad_ref, wgrad_ref,
    ext, feat, grads, tab, taps_rx, mg_tx, mg_rx, taps_in, hspec, spec, conv_tx, conv_rx,
    filt_tx, filt_rx, part_rx,
    halo_send, halo_recv, taps_send, taps_recv, mg_send, mg_recv,
    conv_send, conv_recv, filt_send, filt_recv, part_send, part_recv,
):
    seq_count, ch_count, tok, width = dims
    count = seq_count * ch_count
    length = seq_count * tok
    tiles = width // LANES
    rows_f = length // count
    half_f = rows_f // 2
    ext_rows = tok + HALO
    f32 = jnp.float32
    seq = lax.axis_index("seq")
    ch = lax.axis_index("ch")
    me = seq * ch_count + ch
    scale = length ** (-0.5)

    def place(flat):
        return lax.div(flat, ch_count), lax.rem(flat, ch_count)

    def peer(step):
        return lax.rem(me + step, count)

    def lane_ds(tile):
        return pl.ds(pl.multiple_of(tile * LANES, LANES), LANES)

    barrier = pltpu.get_barrier_semaphore()

    @pl.loop(1, count)
    def _(step):
        pl.semaphore_signal(barrier, inc=1, device_id=place(peer(step)), device_id_type=MESH)

    own = (q_ref, k_ref, v_ref, cot_ref)
    for i, ref in enumerate(own):
        ext[i, HALO : HALO + tok, :] = ref[...]

    @pl.when(seq == 0)
    def _():
        ext[:, 0:HALO, :] = jnp.zeros((4, HALO, width), jnp.bfloat16)

    @pl.when(seq == seq_count - 1)
    def _():
        ext[:, HALO + tok :, :] = jnp.zeros((4, HALO, width), jnp.bfloat16)

    def make_tables(first, last):
        @pl.loop(first, last)
        def _(a):
            rows = pl.ds(pl.multiple_of(a * STEP, STEP), STEP)
            ac = jnp.broadcast_to(ac_ref[pl.ds(a, 1), :], (STEP, LANES))
            an = jnp.broadcast_to(as_ref[pl.ds(a, 1), :], (STEP, LANES))
            for j in range(length // LANES):
                cols = slice(j * LANES, (j + 1) * LANES)
                bc, bs = bc_ref[:, cols], bs_ref[:, cols]
                tab[0, rows, cols], tab[1, rows, cols] = split_parts(ac * bc - an * bs)
                tab[2, rows, cols], tab[3, rows, cols] = split_parts(an * bc + ac * bs)

    blocks = length // STEP + 1
    early = blocks // 2
    make_tables(0, early)
    pl.semaphore_wait(barrier, count - 1)

    def halo_copy(src, dst, i, to):
        return pltpu.make_async_remote_copy(
            src_ref=src, dst_ref=dst, send_sem=halo_send.at[i], recv_sem=halo_recv.at[i],
            device_id=(to, ch), device_id_type=MESH,
        )

    def up_copy(i):
        return halo_copy(own[i].at[tok - HALO :], ext.at[i, 0:HALO], i, seq + 1)

    def down_copy(i):
        return halo_copy(own[i].at[0:HALO], ext.at[i, HALO + tok :], 3 + i, seq - 1)

    @pl.when(seq < seq_count - 1)
    def _():
        for i in range(3):
            up_copy(i).start()

    @pl.when(seq > 0)
    def _():
        for i in range(4):
            down_copy(i).start()

    def taps_copy(step):
        to_seq, to_ch = place(peer(step))
        return pltpu.make_async_remote_copy(
            src_ref=taps_ref.at[:, lane_ds(to_ch * tiles + lax.div(to_seq, 2))],
            dst_ref=taps_rx.at[me], send_sem=taps_send.at[step], recv_sem=taps_recv.at[step],
            device_id=(to_seq, to_ch), device_id_type=MESH,
        )

    @pl.loop(1, count)
    def _(step):
        taps_copy(step).start()

    taps_rx[me] = taps_ref[:, lane_ds(ch * tiles + lax.div(seq, 2))]

    @pl.when(seq > 0)
    def _():
        for i in range(3):
            up_copy(i).wait_recv()

    @pl.when(seq < seq_count - 1)
    def _():
        for i in range(4):
            down_copy(i).wait_recv()

    def mg_copy(to):
        return pltpu.make_async_remote_copy(
            src_ref=mg_tx.at[to], dst_ref=mg_rx.at[seq], send_sem=mg_send.at[to],
            recv_sem=mg_recv.at[seq], device_id=(to, ch), device_id_type=MESH,
        )

    low_tok = low_lanes(tok)

    @pl.loop(0, tiles)
    def _(turn):
        tile = lax.rem(turn + lax.div(seq, 2), tiles)
        cols = lane_ds(tile)
        parts = []
        for i in range(3):
            raw = ext[i, :, cols].astype(f32)
            total = jnp.zeros((ext_rows, LANES), f32)
            for lag in range(TAPS):
                total = total + w_ref[i, lag : lag + 1, cols] * raw[HALO - lag : HALO - lag + ext_rows]
            feat[i, :, cols] = total
            parts.append(total[:tok])
        mix = parts[1] * parts[2]
        gate = ext[3, HALO : HALO + tok, cols].astype(f32) * parts[0]
        even = jnp.where(low_tok, mix, swapped(gate)).astype(jnp.bfloat16)
        odd = jnp.where(low_tok, swapped(mix), gate).astype(jnp.bfloat16)
        for side, value in ((0, even), (1, odd)):
            to = 2 * tile + side
            mg_tx[to] = value

            @pl.when(to != seq)
            def _():
                mg_copy(to).start()

            @pl.when(to == seq)
            def _():
                mg_rx[to] = value

    make_tables(early, blocks)

    @pl.loop(1, count)
    def _(step):
        taps_copy(step).wait_recv()

    odd_side = lax.rem(seq, 2)
    taps_all = taps_rx[...].reshape(length, LANES).astype(f32)
    side_of = jnp.where(low_lanes(length), 0, 1)
    taps_in[...] = jnp.where(side_of == odd_side, taps_all, swapped(taps_all)).astype(jnp.bfloat16)

    chunk = min(2 * LANES, length)

    def row_chunk(i):
        return pl.ds(pl.multiple_of(i * chunk, chunk), chunk)

    @pl.loop(0, length // chunk)
    def _(i):
        rows = row_chunk(i)
        hspec[0, rows, :] = matmul(tab[0, rows, :], taps_in[...]) + matmul(tab[1, rows, :], taps_in[...])
        hspec[1, rows, :] = matmul(tab[2, rows, :], taps_in[...]) + matmul(tab[3, rows, :], taps_in[...])

    def from_peer(copy_of, total, mine):
        @pl.loop(0, total)
        def _(source):
            @pl.when(source != mine)
            def _():
                copy_of(source).wait_recv()

    def mg_arrival(source):
        return pltpu.make_async_remote_copy(
            src_ref=mg_tx.at[source], dst_ref=mg_rx.at[source], send_sem=mg_send.at[source],
            recv_sem=mg_recv.at[source], device_id=(source, ch), device_id_type=MESH,
        )

    from_peer(mg_arrival, seq_count, seq)

    signals = mg_rx.at[...]
    low_chunk = low_lanes(chunk)

    @pl.loop(0, length // chunk)
    def _(i):
        rows = row_chunk(i)
        both = signals[...].reshape(length, LANES)
        xr = matmul(tab[0, rows, :], both) + matmul(tab[1, rows, :], both)
        xs = matmul(tab[2, rows, :], both) + matmul(tab[3, rows, :], both)
        bins = lax.broadcasted_iota(jnp.int32, (chunk, LANES), 0) + i * chunk
        weight = jnp.where(bins == 0, 0.5 / length, 1.0 / length)
        hr = hspec[0, rows, :]
        hs = hspec[1, rows, :]
        wr, ws = xr * weight, xs * weight
        turned = jnp.where(low_chunk, -hs, hs)
        pr = hr * wr + turned * ws
        ps = hr * ws - turned * wr
        other_r, other_s = swapped(xr), swapped(xs)
        fr = wr * other_r + ws * other_s
        fs = wr * other_s - ws * other_r
        for j, value in ((0, pr), (2, ps)):
            spec[j, rows, 0:LANES], spec[j + 1, rows, 0:LANES] = split_parts(value)
        for j, value in ((0, fr), (2, fs)):
            spec[j, rows, LANES:], spec[j + 1, rows, LANES:] = split_parts(value)

    sign_full = 1.0 - 2.0 * lax.rem(lax.broadcasted_iota(jnp.int32, (length, LANES), 0), 2).astype(f32)
    last_x = jnp.sum(mg_rx[...].reshape(length, LANES).astype(f32) * sign_full, axis=0, keepdims=True)
    last_h = jnp.sum(taps_in[...].astype(f32) * sign_full, axis=0, keepdims=True)
    half_weight = 0.5 / length
    last_conv = last_x * last_h * half_weight
    last_filt = last_x * swapped(jnp.broadcast_to(last_x, (8, LANES)))[0:1] * half_weight

    def conv_copy(to):
        return pltpu.make_async_remote_copy(
            src_ref=conv_tx.at[to], dst_ref=conv_rx.at[seq], send_sem=conv_send.at[to],
            recv_sem=conv_recv.at[seq], device_id=(to, ch), device_id_type=MESH,
        )

    def filt_copy(to):
        return pltpu.make_async_remote_copy(
            src_ref=filt_tx.at[to], dst_ref=filt_rx.at[me], send_sem=filt_send.at[to],
            recv_sem=filt_recv.at[me], device_id=place(to), device_id_type=MESH,
        )

    low_half = low_lanes(half_f)
    sign_ext = sign_full[:ext_rows]

    @pl.loop(0, seq_count)
    def _(turn):
        to = lax.rem(seq + 1 + turn, seq_count)
        rows = pl.ds(pl.multiple_of(to * tok, tok), ext_rows)
        out = jnp.zeros((ext_rows, 2 * LANES), f32)
        for j in (0, 2):
            high = tab[j, rows, :]
            out = out + matmul(high, spec[j]) + matmul(high, spec[j + 1]) + matmul(tab[j + 1, rows, :], spec[j])
        conv_tx[to] = (out[:, :LANES] + sign_ext * last_conv).astype(jnp.bfloat16)
        filt = (out[:, LANES:] + sign_ext * last_filt) * scale

        @pl.when(to != seq)
        def _():
            conv_copy(to).start()

        @pl.when(to == seq)
        def _():
            conv_rx[to] = conv_tx[to]

        for c in range(ch_count):
            top = filt[c * rows_f : c * rows_f + half_f]
            bottom = filt[c * rows_f + half_f : (c + 1) * rows_f]
            flat = to * ch_count + c
            filt_tx[flat] = jnp.where(low_half, top, swapped(bottom)).astype(jnp.bfloat16)

            @pl.when(flat != me)
            def _():
                filt_copy(flat).start()

            @pl.when(flat == me)
            def _():
                filt_rx[flat] = filt_tx[flat]

    def conv_arrival(source):
        return pltpu.make_async_remote_copy(
            src_ref=conv_tx.at[source], dst_ref=conv_rx.at[source], send_sem=conv_send.at[source],
            recv_sem=conv_recv.at[source], device_id=(source, ch), device_id_type=MESH,
        )

    from_peer(conv_arrival, seq_count, seq)
    low_ext = low_lanes(ext_rows)
    row_ext = lax.broadcasted_iota(jnp.int32, (ext_rows, LANES), 0)
    keep = jnp.logical_or(row_ext < tok, seq < seq_count - 1)

    @pl.loop(0, tiles)
    def _(tile):
        cols = lane_ds(tile)
        first = jnp.where(keep, conv_rx[2 * tile].astype(f32), 0.0)
        second = jnp.where(keep, conv_rx[2 * tile + 1].astype(f32), 0.0)
        conv = jnp.where(low_ext, first, swapped(second))
        mix_grad = jnp.where(low_ext, swapped(first), second)
        mixed_ref[:, cols] = (feat[0, :tok, cols] * conv[:tok]).astype(jnp.bfloat16)
        terms = (
            ext[3, HALO:, cols].astype(f32) * conv,
            mix_grad * feat[2, :, cols],
            mix_grad * feat[1, :, cols],
        )
        for i in range(3):
            grads[i, :, cols] = terms[i]
            raw = ext[i, :, cols].astype(f32)
            sums = [
                jnp.sum(terms[i][:tok] * raw[HALO - lag : HALO - lag + tok], axis=0, keepdims=True)
                for lag in range(TAPS)
            ]
            sums.append(jnp.zeros((1, LANES), f32))
            part_rx[seq, 8 * i : 8 * i + 8, cols] = jnp.concatenate(sums, axis=0)

    def part_copy(step):
        to = lax.rem(seq + step, seq_count)
        return pltpu.make_async_remote_copy(
            src_ref=part_rx.at[seq], dst_ref=part_rx.at[seq], send_sem=part_send.at[to],
            recv_sem=part_recv.at[seq], device_id=(to, ch), device_id_type=MESH,
        )

    @pl.loop(1, seq_count)
    def _(step):
        part_copy(step).start()

    @pl.loop(0, tiles)
    def _(tile):
        cols = lane_ds(tile)
        for i, ref in enumerate((qg_ref, kg_ref, vg_ref)):
            term = grads[i, :, cols]
            total = jnp.zeros((tok, LANES), f32)
            for lag in range(TAPS):
                total = total + w_ref[i, lag : lag + 1, cols] * term[lag : lag + tok]
            ref[:, cols] = total.astype(jnp.bfloat16)

    def filt_arrival(source):
        return pltpu.make_async_remote_copy(
            src_ref=filt_tx.at[source], dst_ref=filt_rx.at[source], send_sem=filt_send.at[source],
            recv_sem=filt_recv.at[source], device_id=place(source), device_id_type=MESH,
        )

    from_peer(filt_arrival, count, me)

    @pl.loop(0, ch_count * tiles)
    def _(tile):
        cols = lane_ds(tile)
        pair = lax.rem(tile, tiles)
        owner = lax.div(tile, tiles)
        first = filt_rx[2 * pair * ch_count + owner].astype(f32)
        second = filt_rx[(2 * pair + 1) * ch_count + owner].astype(f32)
        fgrad_ref[0:half_f, cols] = jnp.where(low_half, first, swapped(second))
        fgrad_ref[half_f:rows_f, cols] = jnp.where(low_half, swapped(first), second)

    def part_arrival(source):
        return pltpu.make_async_remote_copy(
            src_ref=part_rx.at[seq], dst_ref=part_rx.at[source], send_sem=part_send.at[source],
            recv_sem=part_recv.at[source], device_id=(source, ch), device_id_type=MESH,
        )

    from_peer(part_arrival, seq_count, seq)
    whole = part_rx[0]
    for source in range(1, seq_count):
        whole = whole + part_rx[source]
    whole = whole * scale
    for i in range(3):
        wgrad_ref[i] = whole[8 * i : 8 * i + TAPS]

    @pl.when(seq < seq_count - 1)
    def _():
        for i in range(3):
            up_copy(i).wait_send()

    @pl.when(seq > 0)
    def _():
        for i in range(4):
            down_copy(i).wait_send()

    @pl.loop(1, count)
    def _(step):
        taps_copy(step).wait_send()
        filt_copy(peer(step)).wait_send()

    @pl.loop(1, seq_count)
    def _(step):
        to = lax.rem(seq + step, seq_count)
        mg_copy(to).wait_send()
        conv_copy(to).wait_send()
        part_copy(step).wait_send()


def on_device(dims, *args):
    seq_count, ch_count, tok, width = dims
    count = seq_count * ch_count
    length = seq_count * tok
    half_f = length // count // 2
    bf16, f32 = jnp.bfloat16, jnp.float32
    vmem = pl.BlockSpec(memory_space=pltpu.VMEM)
    ext_rows = tok + HALO
    dma = pltpu.SemaphoreType.DMA
    out = jax.ShapeDtypeStruct((tok, width), bf16)
    return pl.pallas_call(
        functools.partial(operator_kernel, dims),
        out_shape=(
            out, out, out, out,
            jax.ShapeDtypeStruct((length // count, width * ch_count), f32),
            jax.ShapeDtypeStruct((3, TAPS, width), f32),
        ),
        in_specs=[vmem] * 10,
        out_specs=(vmem,) * 6,
        scratch_shapes=[
            pltpu.VMEM((4, tok + 2 * HALO, width), bf16),
            pltpu.VMEM((3, ext_rows, width), f32),
            pltpu.VMEM((3, ext_rows, width), f32),
            pltpu.VMEM((4, length + STEP, length), bf16),
            pltpu.VMEM((count, 2 * half_f, LANES), bf16),
            pltpu.VMEM((seq_count, tok, LANES), bf16),
            pltpu.VMEM((seq_count, tok, LANES), bf16),
            pltpu.VMEM((length, LANES), bf16),
            pltpu.VMEM((2, length, LANES), f32),
            pltpu.VMEM((4, length, 2 * LANES), bf16),
            pltpu.VMEM((seq_count, ext_rows, LANES), bf16),
            pltpu.VMEM((seq_count, ext_rows, LANES), bf16),
            pltpu.VMEM((count, half_f, LANES), bf16),
            pltpu.VMEM((count, half_f, LANES), bf16),
            pltpu.VMEM((seq_count, 24, width), f32),
            dma((7,)), dma((7,)), dma((count,)), dma((count,)),
            dma((seq_count,)), dma((seq_count,)), dma((seq_count,)), dma((seq_count,)),
            dma((count,)), dma((count,)), dma((seq_count,)), dma((seq_count,)),
        ],
        compiler_params=pltpu.CompilerParams(collective_id=0, has_side_effects=True),
    )(*args, *angle_tables(length))


def block_function(mesh, query_raw, filter_taps):
    seq_count, ch_count = mesh.shape["seq"], mesh.shape["ch"]
    tok, width = query_raw.shape
    length = seq_count * tok
    rows_f = filter_taps.shape[0]
    fits = (
        2 * width == seq_count * LANES
        and seq_count % 2 == 0
        and tok % LANES == 0
        and length % (2 * LANES) == 0
        and length <= 2048
        and rows_f % 32 == 0
    )
    if fits:
        return functools.partial(on_device, (seq_count, ch_count, tok, width))
    return on_device_large


def solution(mesh):
    def body(*args):
        return block_function(mesh, args[0], args[4])(*args)

    return jax.shard_map(
        body,
        mesh=mesh,
        in_specs=(
            P("seq", "ch"),
            P("seq", "ch"),
            P("seq", "ch"),
            P(None, None, "ch"),
            P(("seq", "ch"), None),
            P("seq", "ch"),
        ),
        out_specs=(
            P("seq", "ch"),
            P("seq", "ch"),
            P("seq", "ch"),
            P("seq", "ch"),
            P(("seq", "ch"), None),
            P(None, None, "ch"),
        ),
        check_vma=False,
    )
```

profile of v0, /device:TPU:0, one launch (start us, length us, event | category | flops | bytes accessed | tf_op | source)
XLA Modules:
  0.0 53.6 jit_solution(11893201072395216285)
XLA Ops:
  0.6 47.7 %shard_map.145 = (bf16[128,512]{1,0:T(8,128)(2,1)}, bf16[128,512]{1,0:T(8,128)(2,1)}, bf16[128,512]{1,0:T(8,128)(2,1)}, bf16[128,512]{1,0:T(8,128)(2,1)}, f32[32,2048]{1,0:T(8,128)}, /*index=5*/f32[3,7,512]{2,1,0:T(8,128)}) custom-call(bf16[128,512]{1,0:T(8,128)(2,1)} %q_ref.1, bf16[128,512]{1,0:T(8,128)(2,1)} %k_ref.1, bf16[128,512]{1,0:T(8,128)(2,1)} %v_ref.1, ...), custom_call_target="tpu_custom_call" | custom-call | tf_op jit(solution)/shard_map/pallas_call | solution.py:630
  48.3 0.0 copy-start.3
  48.3 1.6 %copy.22 = bf16[128,512]{1,0:T(8,128)(2,1)} copy(bf16[128,512]{1,0:T(8,128)(2,1)} %get-tuple-element.12) | data formatting | bytes 262144
  49.9 0.0 copy-done.3
  49.9 0.0 copy-start.2
  49.9 0.0 copy-start.1
  49.9 0.7 %copy.23 = bf16[128,512]{1,0:T(8,128)(2,1)} copy(bf16[128,512]{1,0:T(8,128)(2,1)S(1)} %copy-done.3) | data formatting | bytes 262144
  50.6 0.3 copy-done.2
  50.9 0.0 copy-start
  50.9 0.7 %copy.24 = bf16[128,512]{1,0:T(8,128)(2,1)} copy(bf16[128,512]{1,0:T(8,128)(2,1)S(1)} %copy-done.2) | data formatting | bytes 262144
  51.5 0.0 copy-done.1
  51.5 0.7 %copy.25 = bf16[128,512]{1,0:T(8,128)(2,1)} copy(bf16[128,512]{1,0:T(8,128)(2,1)S(1)} %copy-done.1) | data formatting | bytes 262144
  52.2 0.0 copy-done
  52.2 0.0 copy-start.4
  52.2 0.7 %copy.26 = f32[32,2048]{1,0:T(8,128)} copy(f32[32,2048]{1,0:T(8,128)S(1)} %copy-done) | data formatting | bytes 524288
  52.9 0.1 copy-done.4
  53.0 0.6 %copy.27 = f32[3,7,512]{2,1,0:T(8,128)} copy(f32[3,7,512]{2,1,0:T(8,128)S(1)} %copy-done.4) | data formatting | bytes 86016
Async XLA Ops:
  48.3 1.6 %copy-start.3 = (bf16[128,512]{1,0:T(8,128)(2,1)S(1)}, bf16[128,512]{1,0:T(8,128)(2,1)}, u32[]{:S(2)}) copy-start(bf16[128,512]{1,0:T(8,128)(2,1)} %get-tuple-element.13) | copy-start | bytes 393220
  49.9 1.0 %copy-start.2 = (bf16[128,512]{1,0:T(8,128)(2,1)S(1)}, bf16[128,512]{1,0:T(8,128)(2,1)}, u32[]{:S(2)}) copy-start(bf16[128,512]{1,0:T(8,128)(2,1)} %get-tuple-element.14) | copy-start | bytes 393220
  49.9 1.6 %copy-start.1 = (bf16[128,512]{1,0:T(8,128)(2,1)S(1)}, bf16[128,512]{1,0:T(8,128)(2,1)}, u32[]{:S(2)}) copy-start(bf16[128,512]{1,0:T(8,128)(2,1)} %get-tuple-element.15) | copy-start | bytes 393220
  50.9 1.3 %copy-start = (f32[32,2048]{1,0:T(8,128)S(1)}, f32[32,2048]{1,0:T(8,128)}, u32[]{:S(2)}) copy-start(f32[32,2048]{1,0:T(8,128)} %get-tuple-element.16) | copy-start | bytes 786436
  52.2 0.8 %copy-start.4 = (f32[3,7,512]{2,1,0:T(8,128)S(1)}, f32[3,7,512]{2,1,0:T(8,128)}, u32[]{:S(2)}) copy-start(f32[3,7,512]{2,1,0:T(8,128)} %get-tuple-element.17) | copy-start | bytes 129028
where the time goes:
time: 54 us; the launch traced here: 53.6 us
  Pallas kernels  47.7 us (88%)
  local copies, waits for them, and re-layouts  5.29 us (10%)
  between operations  0.66 us (1%)
    pallas_call x1, Pallas kernels, on_device(): pl.pallas_call(functools.partial(operator_kernel, dims), out_shape=(out,...  47.7 us
    unnamed x16, local copies, waits for them, and re-layouts  5.29 us

commit v1 on v0

--- a/solution.py
+++ b/solution.py
@@ -210,6 +210,8 @@
 LANES = 128
 HALO = 16
 STEP = 32
+SPLIT = (TAPS + 1) // 2
+PART_ROWS = 16
 MESH = pl.DeviceIdType.MESH
 
 
@@ -246,10 +248,10 @@
     dims,
     q_ref, k_ref, v_ref, w_ref, taps_ref, cot_ref, ac_ref, as_ref, bc_ref, bs_ref,
     mixed_ref, qg_ref, kg_ref, vg_ref, fgrad_ref, wgrad_ref,
-    ext, feat, grads, tab, taps_rx, mg_tx, mg_rx, taps_in, hspec, spec, conv_tx, conv_rx,
-    filt_tx, filt_rx, part_rx,
+    ext, feat, grads, tab, taps_tx, taps_rx, mg_tx, mg_rx, taps_in, hspec, spec, conv_tx, conv_rx,
+    filt_tx, filt_rx, part_tx, part_rx, sums_rx,
     halo_send, halo_recv, taps_send, taps_recv, mg_send, mg_recv,
-    conv_send, conv_recv, filt_send, filt_recv, part_send, part_recv,
+    conv_send, conv_recv, filt_send, filt_recv, part_send, part_recv, sum_send, sum_recv,
 ):
     seq_count, ch_count, tok, width = dims
     count = seq_count * ch_count
@@ -279,6 +281,17 @@
     def _(step):
         pl.semaphore_signal(barrier, inc=1, device_id=place(peer(step)), device_id_type=MESH)
 
+    low_half = low_lanes(half_f)
+
+    @pl.loop(0, ch_count * tiles)
+    def _(tile):
+        cols = lane_ds(tile)
+        top = taps_ref[0:half_f, cols].astype(f32)
+        bottom = taps_ref[half_f:rows_f, cols].astype(f32)
+        even_flat = 2 * lax.rem(tile, tiles) * ch_count + lax.div(tile, tiles)
+        taps_tx[even_flat] = jnp.where(low_half, top, swapped(bottom)).astype(jnp.bfloat16)
+        taps_tx[even_flat + ch_count] = jnp.where(low_half, swapped(top), bottom).astype(jnp.bfloat16)
+
     own = (q_ref, k_ref, v_ref, cot_ref)
     for i, ref in enumerate(own):
         ext[i, HALO : HALO + tok, :] = ref[...]
@@ -333,7 +346,7 @@
     def taps_copy(step):
         to_seq, to_ch = place(peer(step))
         return pltpu.make_async_remote_copy(
-            src_ref=taps_ref.at[:, lane_ds(to_ch * tiles + lax.div(to_seq, 2))],
+            src_ref=taps_tx.at[peer(step)],
             dst_ref=taps_rx.at[me], send_sem=taps_send.at[step], recv_sem=taps_recv.at[step],
             device_id=(to_seq, to_ch), device_id_type=MESH,
         )
@@ -342,7 +355,7 @@
     def _(step):
         taps_copy(step).start()
 
-    taps_rx[me] = taps_ref[:, lane_ds(ch * tiles + lax.div(seq, 2))]
+    taps_rx[me] = taps_tx[me]
 
     @pl.when(seq > 0)
     def _():
@@ -396,10 +409,12 @@
     def _(step):
         taps_copy(step).wait_recv()
 
-    odd_side = lax.rem(seq, 2)
-    taps_all = taps_rx[...].reshape(length, LANES).astype(f32)
-    side_of = jnp.where(low_lanes(length), 0, 1)
-    taps_in[...] = jnp.where(side_of == odd_side, taps_all, swapped(taps_all)).astype(jnp.bfloat16)
+    low_count = low_lanes(count * half_f)
+    taps_all = taps_rx[...].reshape(count * half_f, LANES).astype(f32)
+    taps_turned = swapped(taps_all)
+    for side, pair in enumerate(((taps_all, taps_turned), (taps_turned, taps_all))):
+        value = jnp.where(low_count, *pair).astype(jnp.bfloat16)
+        taps_in[:, side * half_f : (side + 1) * half_f, :] = value.reshape(count, half_f, LANES)
 
     chunk = min(2 * LANES, length)
 
@@ -409,8 +424,8 @@
     @pl.loop(0, length // chunk)
     def _(i):
         rows = row_chunk(i)
-        hspec[0, rows, :] = matmul(tab[0, rows, :], taps_in[...]) + matmul(tab[1, rows, :], taps_in[...])
-        hspec[1, rows, :] = matmul(tab[2, rows, :], taps_in[...]) + matmul(tab[3, rows, :], taps_in[...])
+        hspec[0, rows, :] = matmul(tab[0, rows, :], taps_in[...].reshape(length, LANES)) + matmul(tab[1, rows, :], taps_in[...].reshape(length, LANES))
+        hspec[1, rows, :] = matmul(tab[2, rows, :], taps_in[...].reshape(length, LANES)) + matmul(tab[3, rows, :], taps_in[...].reshape(length, LANES))
 
     def from_peer(copy_of, total, mine):
         @pl.loop(0, total)
@@ -454,7 +469,7 @@
 
     sign_full = 1.0 - 2.0 * lax.rem(lax.broadcasted_iota(jnp.int32, (length, LANES), 0), 2).astype(f32)
     last_x = jnp.sum(mg_rx[...].reshape(length, LANES).astype(f32) * sign_full, axis=0, keepdims=True)
-    last_h = jnp.sum(taps_in[...].astype(f32) * sign_full, axis=0, keepdims=True)
+    last_h = jnp.sum(taps_in[...].reshape(length, LANES).astype(f32) * sign_full, axis=0, keepdims=True)
     half_weight = 0.5 / length
     last_conv = last_x * last_h * half_weight
     last_filt = last_x * swapped(jnp.broadcast_to(last_x, (8, LANES)))[0:1] * half_weight
@@ -471,7 +486,6 @@
             recv_sem=filt_recv.at[me], device_id=place(to), device_id_type=MESH,
         )
 
-    low_half = low_lanes(half_f)
     sign_ext = sign_full[:ext_rows]
 
     @pl.loop(0, seq_count)
@@ -499,13 +513,12 @@
             flat = to * ch_count + c
             filt_tx[flat] = jnp.where(low_half, top, swapped(bottom)).astype(jnp.bfloat16)
 
-            @pl.when(flat != me)
-            def _():
-                filt_copy(flat).start()
-
-            @pl.when(flat == me)
-            def _():
-                filt_rx[flat] = filt_tx[flat]
+
+    filt_rx[me] = filt_tx[me]
+
+    @pl.loop(1, count)
+    def _(step):
+        filt_copy(peer(step)).start()
 
     def conv_arrival(source):
         return pltpu.make_async_remote_copy(
@@ -517,6 +530,12 @@
     low_ext = low_lanes(ext_rows)
     row_ext = lax.broadcasted_iota(jnp.int32, (ext_rows, LANES), 0)
     keep = jnp.logical_or(row_ext < tok, seq < seq_count - 1)
+
+    def part_copy(to):
+        return pltpu.make_async_remote_copy(
+            src_ref=part_tx.at[to], dst_ref=part_rx.at[seq], send_sem=part_send.at[to],
+            recv_sem=part_recv.at[seq], device_id=(to, ch), device_id_type=MESH,
+        )
 
     @pl.loop(0, tiles)
     def _(tile):
@@ -531,6 +550,7 @@
             mix_grad * feat[2, :, cols],
             mix_grad * feat[1, :, cols],
         )
+        lags = []
         for i in range(3):
             grads[i, :, cols] = terms[i]
             raw = ext[i, :, cols].astype(f32)
@@ -538,19 +558,20 @@
                 jnp.sum(terms[i][:tok] * raw[HALO - lag : HALO - lag + tok], axis=0, keepdims=True)
                 for lag in range(TAPS)
             ]
-            sums.append(jnp.zeros((1, LANES), f32))
-            part_rx[seq, 8 * i : 8 * i + 8, cols] = jnp.concatenate(sums, axis=0)
-
-    def part_copy(step):
-        to = lax.rem(seq + step, seq_count)
-        return pltpu.make_async_remote_copy(
-            src_ref=part_rx.at[seq], dst_ref=part_rx.at[seq], send_sem=part_send.at[to],
-            recv_sem=part_recv.at[seq], device_id=(to, ch), device_id_type=MESH,
-        )
-
-    @pl.loop(1, seq_count)
-    def _(step):
-        part_copy(step).start()
+            lags.append(sums)
+        for side in range(2):
+            picked = [row for sums in lags for row in sums[side * SPLIT : (side + 1) * SPLIT]]
+            picked.append(jnp.zeros((PART_ROWS - len(picked), LANES), f32))
+            to = 2 * tile + side
+            part_tx[to] = jnp.concatenate(picked, axis=0)
+
+            @pl.when(to != seq)
+            def _():
+                part_copy(to).start()
+
+            @pl.when(to == seq)
+            def _():
+                part_rx[to] = part_tx[to]
 
     @pl.loop(0, tiles)
     def _(tile):
@@ -562,6 +583,28 @@
                 total = total + w_ref[i, lag : lag + 1, cols] * term[lag : lag + tok]
             ref[:, cols] = total.astype(jnp.bfloat16)
 
+    def part_arrival(source):
+        return pltpu.make_async_remote_copy(
+            src_ref=part_tx.at[source], dst_ref=part_rx.at[source], send_sem=part_send.at[source],
+            recv_sem=part_recv.at[source], device_id=(source, ch), device_id_type=MESH,
+        )
+
+    from_peer(part_arrival, seq_count, seq)
+    own_sum = part_rx[0]
+    for source in range(1, seq_count):
+        own_sum = own_sum + part_rx[source]
+    sums_rx[seq] = own_sum * scale
+
+    def sum_copy(to):
+        return pltpu.make_async_remote_copy(
+            src_ref=sums_rx.at[seq], dst_ref=sums_rx.at[seq], send_sem=sum_send.at[to],
+            recv_sem=sum_recv.at[seq], device_id=(to, ch), device_id_type=MESH,
+        )
+
+    @pl.loop(1, seq_count)
+    def _(step):
+        sum_copy(lax.rem(seq + step, seq_count)).start()
+
     def filt_arrival(source):
         return pltpu.make_async_remote_copy(
             src_ref=filt_tx.at[source], dst_ref=filt_rx.at[source], send_sem=filt_send.at[source],
@@ -580,19 +623,21 @@
         fgrad_ref[0:half_f, cols] = jnp.where(low_half, first, swapped(second))
         fgrad_ref[half_f:rows_f, cols] = jnp.where(low_half, swapped(first), second)
 
-    def part_arrival(source):
-        return pltpu.make_async_remote_copy(
-            src_ref=part_rx.at[seq], dst_ref=part_rx.at[source], send_sem=part_send.at[source],
-            recv_sem=part_recv.at[source], device_id=(source, ch), device_id_type=MESH,
-        )
-
-    from_peer(part_arrival, seq_count, seq)
-    whole = part_rx[0]
-    for source in range(1, seq_count):
-        whole = whole + part_rx[source]
-    whole = whole * scale
-    for i in range(3):
-        wgrad_ref[i] = whole[8 * i : 8 * i + TAPS]
+    def sum_arrival(source):
+        return pltpu.make_async_remote_copy(
+            src_ref=sums_rx.at[seq], dst_ref=sums_rx.at[source], send_sem=sum_send.at[source],
+            recv_sem=sum_recv.at[source], device_id=(source, ch), device_id_type=MESH,
+        )
+
+    from_peer(sum_arrival, seq_count, seq)
+    for tile in range(tiles):
+        cols = slice(tile * LANES, (tile + 1) * LANES)
+        for side in range(2):
+            rows = min(SPLIT, TAPS - side * SPLIT)
+            for i in range(3):
+                wgrad_ref[i, side * SPLIT : side * SPLIT + rows, cols] = sums_rx[
+                    2 * tile + side, i * rows : (i + 1) * rows
+                ]
 
     @pl.when(seq < seq_count - 1)
     def _():
@@ -614,7 +659,14 @@
         to = lax.rem(seq + step, seq_count)
         mg_copy(to).wait_send()
         conv_copy(to).wait_send()
-        part_copy(step).wait_send()
+        part_copy(to).wait_send()
+        sum_copy(to).wait_send()
+
+
+def write_out(*refs):
+    half = len(refs) // 2
+    for source, target in zip(refs[:half], refs[half:]):
+        target[...] = source[...]
 
 
 def on_device(dims, *args):
@@ -627,13 +679,14 @@
     ext_rows = tok + HALO
     dma = pltpu.SemaphoreType.DMA
     out = jax.ShapeDtypeStruct((tok, width), bf16)
-    return pl.pallas_call(
+    outs = (
+        out, out, out, out,
+        jax.ShapeDtypeStruct((length // count, width * ch_count), f32),
+        jax.ShapeDtypeStruct((3, TAPS, width), f32),
+    )
+    results = pl.pallas_call(
         functools.partial(operator_kernel, dims),
-        out_shape=(
-            out, out, out, out,
-            jax.ShapeDtypeStruct((length // count, width * ch_count), f32),
-            jax.ShapeDtypeStruct((3, TAPS, width), f32),
-        ),
+        out_shape=outs,
         in_specs=[vmem] * 10,
         out_specs=(vmem,) * 6,
         scratch_shapes=[
@@ -641,23 +694,30 @@
             pltpu.VMEM((3, ext_rows, width), f32),
             pltpu.VMEM((3, ext_rows, width), f32),
             pltpu.VMEM((4, length + STEP, length), bf16),
-            pltpu.VMEM((count, 2 * half_f, LANES), bf16),
+            pltpu.VMEM((count, half_f, LANES), bf16),
+            pltpu.VMEM((count, half_f, LANES), bf16),
             pltpu.VMEM((seq_count, tok, LANES), bf16),
             pltpu.VMEM((seq_count, tok, LANES), bf16),
-            pltpu.VMEM((length, LANES), bf16),
+            pltpu.VMEM((count, 2 * half_f, LANES), bf16),
             pltpu.VMEM((2, length, LANES), f32),
             pltpu.VMEM((4, length, 2 * LANES), bf16),
             pltpu.VMEM((seq_count, ext_rows, LANES), bf16),
             pltpu.VMEM((seq_count, ext_rows, LANES), bf16),
             pltpu.VMEM((count, half_f, LANES), bf16),
             pltpu.VMEM((count, half_f, LANES), bf16),
-            pltpu.VMEM((seq_count, 24, width), f32),
+            pltpu.VMEM((seq_count, PART_ROWS, LANES), f32),
+            pltpu.VMEM((seq_count, PART_ROWS, LANES), f32),
+            pltpu.VMEM((seq_count, PART_ROWS, LANES), f32),
             dma((7,)), dma((7,)), dma((count,)), dma((count,)),
             dma((seq_count,)), dma((seq_count,)), dma((seq_count,)), dma((seq_count,)),
             dma((count,)), dma((count,)), dma((seq_count,)), dma((seq_count,)),
+            dma((seq_count,)), dma((seq_count,)),
         ],
         compiler_params=pltpu.CompilerParams(collective_id=0, has_side_effects=True),
     )(*args, *angle_tables(length))
+    return pl.pallas_call(
+        write_out, out_shape=outs, in_specs=[vmem] * 6, out_specs=(vmem,) * 6
+    )(*results)
 
 
 def block_function(mesh, query_raw, filter_taps):

time: 54 us -> 50.3 us (0.931)
  local copies, waits for them, and re-layouts: 5.29 us -> 0 us
  Pallas kernels: 47.7 us -> 49.5 us
    unnamed x16 -> x0, local copies, waits for them, and re-layouts: 5.29 us -> none
    pallas_call x1 -> x2, Pallas kernels: 47.7 us -> 49.5 us  [the longest x1 47.4 us: on_device(): pl.pallas_call(functools.partial(operator_kernel, dims), out_shape=outs,...]
where the time goes in v1:
time: 50.3 us; the launch traced here: 50.2 us
  Pallas kernels  49.5 us (98%)
  between operations  0.64 us (1%)
    pallas_call x1, Pallas kernels, on_device(): pl.pallas_call(functools.partial(operator_kernel, dims), out_shape=outs,...  47.4 us
    pallas_call x1, Pallas kernels, on_device(): pl.pallas_call(write_out, out_shape=outs, in_specs=[vmem] * 6, out_specs=...  2.11 us

profile of v1, /device:TPU:0, one launch (start us, length us, event | category | flops | bytes accessed | tf_op | source)
XLA Modules:
  0.0 50.2 jit_solution(3384380071728537617)
XLA Ops:
  0.6 47.4 %shard_map.145 = (bf16[128,512]{1,0:T(8,128)(2,1)}, bf16[128,512]{1,0:T(8,128)(2,1)}, bf16[128,512]{1,0:T(8,128)(2,1)}, bf16[128,512]{1,0:T(8,128)(2,1)}, f32[32,2048]{1,0:T(8,128)}, /*index=5*/f32[3,7,512]{2,1,0:T(8,128)}) custom-call(bf16[128,512]{1,0:T(8,128)(2,1)} %q_ref.1, bf16[128,512]{1,0:T(8,128)(2,1)} %k_ref.1, bf16[128,512]{1,0:T(8,128)(2,1)} %v_ref.1, ...), custom_call_target="tpu_custom_call" | custom-call | tf_op jit(solution)/shard_map/pallas_call | solution.py:687
  48.0 2.1 %shard_map.146 = (bf16[128,512]{1,0:T(8,128)(2,1)}, bf16[128,512]{1,0:T(8,128)(2,1)}, bf16[128,512]{1,0:T(8,128)(2,1)}, bf16[128,512]{1,0:T(8,128)(2,1)}, f32[32,2048]{1,0:T(8,128)}, /*index=5*/f32[3,7,512]{2,1,0:T(8,128)}) custom-call(bf16[128,512]{1,0:T(8,128)(2,1)} %get-tuple-element.12.refs_0_, bf16[128,512]{1,0:T(8,128)(2,1)} %get-tuple-element.13.refs_1_, ...), custom_call_target="tpu_custom_call" | custom-call | tf_op jit(solution)/shard_map/pallas_call | solution.py:718
